TPU v7x, 256 devices: a whole 4x4x8 slice. The times are simulated.
256 devices in a mesh: row: 16 (over z_hi, y), col: 16 (over x, z_lo, core).
Axes of the slice: x: 4, y: 4, z: 8 (z_hi: 4, z_lo: 2; z = z_hi * 2 + z_lo), core: 2. Of those that a mesh axis runs over, the one named last changes fastest.
Arguments:
- positions: float32 [3, 32768], P(None, ('row', 'col')), may hold values from 0 to 1
- radii: float32 [32768], P(('row', 'col')), may hold values from 0.5 to 2
- right_side: float32 [32768, 256], P(('row', 'col')), may hold values from -60 to 60, as said below
Outputs:
- solution: float32 [32768, 256], P(('row', 'col'))
- residual: float32 [32768, 256], P(('row', 'col'))
Inputs may be any that keep to these rules, and one draw needn't show every extreme that they name: `right_side`: real values of varying scale.
All inputs are finite; a program needn't handle non-finite values.
Results may differ from a plain program's by a relative error of at most 0.0003.
Values sent between devices are 32-bit elements; how exact they have to be, the bound alone decides.
A program may use at most 64 MiB of HBM per device.

v0:
```python
import jax
import jax.numpy as jnp
from jax import lax
from jax.sharding import PartitionSpec as P

ITERS = 2


def kernel_product(row_points, col_points, values, kernel_scale, softening, limit):
    row_count = row_points.shape[1]
    col_count = col_points.shape[1]
    blocks = max(1, row_count * col_count // limit)
    while row_count % blocks:
        blocks = blocks - 1
    block_size = row_count // blocks
    grouped = row_points.reshape(3, blocks, block_size).transpose(1, 0, 2)

    def apply_block(row_block):
        first = row_block[0][:, None] - col_points[0][None, :]
        second = row_block[1][:, None] - col_points[1][None, :]
        third = row_block[2][:, None] - col_points[2][None, :]
        squared = first * first + second * second + third * third
        weights = lax.rsqrt(squared + softening) * kernel_scale
        return jnp.dot(
            weights, values, preferred_element_type=jnp.float32, precision=lax.Precision.HIGHEST
        )

    return lax.map(apply_block, grouped).reshape(row_count, values.shape[1])


def constants(total):
    kernel_scale = float(total) ** (-0.5)
    spacing = 0.25 * float(total) ** (-1.0 / 3.0)
    return (kernel_scale, spacing * spacing)


def squares(residual):
    return lax.psum(jnp.sum(residual * residual, axis=0), ("row", "col"))


def body(positions, radii, right_side):
    local_count = positions.shape[1]
    total = local_count * lax.axis_size("row") * lax.axis_size("col")
    kernel_scale, softening = constants(total)
    row_points = lax.all_gather(positions, "col", axis=1, tiled=True)
    col_points = lax.all_gather(positions, "row", axis=1, tiled=True)
    limit = 1 << 20
    solution = jnp.zeros_like(right_side)
    residual = right_side
    direction = right_side
    norm_now = squares(residual)
    for iteration in range(ITERS):
        col_values = lax.all_gather(direction, "row", axis=0, tiled=True)
        summed = lax.psum_scatter(
            kernel_product(row_points, col_points, col_values, kernel_scale, softening, limit),
            "col",
            scatter_dimension=0,
            tiled=True,
        )
        image_vec = direction / radii[:, None] + summed
        curvature = lax.psum(jnp.sum(direction * image_vec, axis=0), ("row", "col"))
        step_size = norm_now / curvature
        solution = solution + step_size * direction
        residual = residual - step_size * image_vec
        if iteration + 1 < ITERS:
            norm_next = squares(residual)
            direction = residual + norm_next / norm_now * direction
            norm_now = norm_next
    return (solution, residual)


def solution(mesh):
    return jax.shard_map(
        body,
        mesh=mesh,
        in_specs=(P(None, ("row", "col")), P(("row", "col")), P(("row", "col"), None)),
        out_specs=(P(("row", "col"), None), P(("row", "col"), None)),
        check_vma=False,
    )
```

profile of v0, /device:TPU:1, one launch (start us, length us, event | category | flops | bytes accessed | tf_op | source)
XLA Modules:
  0.0 550.6 jit_solution(2993443880854321543)
XLA Ops:
  7.2 0.0 all-gather.3.cloned.1.call-start
  7.2 0.7 all-gather.3.cloned.1.call-update
  7.9 0.0 reduce-scatter.3.cloned.1.call-start
  7.9 40.7 %all_gather.13 = f32[3,2048]{1,0:T(4,128)S(1)} all-gather(f32[3,128]{1,0:T(4,128)} %param.7), channel_id=1, replica_groups=mesh['row'=16,'col'=16] {'row'}, dimensions={1}, use_global_device_ids=true | all-gather | bytes 26112 | tf_op jit(solution)/shard_map/all_gather | solution.py:46
  48.7 28.0 %all_gather.12 = f32[3,2048]{1,0:T(4,128)S(1)} all-gather(f32[3,128]{1,0:T(4,128)} %param.7), channel_id=1, replica_groups=mesh['row'=16,'col'=16] {'col'}, dimensions={1}, use_global_device_ids=true | all-gather | bytes 26112 | tf_op jit(solution)/shard_map/all_gather | solution.py:45
  76.6 0.0 all-gather.3.cloned.1.call-done
  76.6 0.2 broadcast.19.clone
  76.8 25.9 %while.20 = (s32[]{:T(128)}, f32[4,512,256]{2,1,0:T(8,128)S(1)}, f32[4,3,512]{2,1,0:T(4,128)S(1)}, f32[3,2048]{1,0:T(4,128)S(1)}, f32[2048,256]{1,0:T(8,128)}, /*index=5*/s32[]{:T(128)}, s32[]{:T(128)}, s32[]{}, s32[]{}) while((s32[]{:T(128)}, f32[4,512,256]{2,1,0:T(8,128)S(1)}, f32[4,3,512]{2,1,0:T(4,128)S(1)}, f32[3,2048]{1,0:T(4,128)S(1)}, ...), condition=%wide.region_3.4_spmd, body=%wide.region_2.3_spmd.sunk | while | flops 3231711232 | bytes 2713733 | solution.py:28
  76.8 6.4 %fusion.71 = f32[4,512,256]{2,1,0:T(8,128)S(1)} fusion(f32[4,512,256]{2,1,0:T(8,128)S(1)} %get-tuple-element.194, s32[]{:T(128)} %get-tuple-element.193, f32[2048,256]{1,0:T(8,128)} %get-tuple-element.206, f32[2048]{0:T(1024)S(1)} %bitcast.63, f32[512]{0:T(512)S(1)} %bitcast.70, f32[2048]{0:T(1024)S(1)} %bitcast.64, f32[512]{0:T(512)S(1)} %bitcast.69, ...), kind=kOutput, calls=%fused_computation.21.clone.1 | convolution fusion | flops 3231711232 | bytes 2652164 | tf_op jit(solution)/shard_map/while/body/eval_jaxpr/dot_general | solution.py:24
  83.3 6.4 %fusion.71 = f32[4,512,256]{2,1,0:T(8,128)S(1)} fusion(f32[4,512,256]{2,1,0:T(8,128)S(1)} %get-tuple-element.194, s32[]{:T(128)} %get-tuple-element.193, f32[2048,256]{1,0:T(8,128)} %get-tuple-element.206, f32[2048]{0:T(1024)S(1)} %bitcast.63, f32[512]{0:T(512)S(1)} %bitcast.70, f32[2048]{0:T(1024)S(1)} %bitcast.64, f32[512]{0:T(512)S(1)} %bitcast.69, ...), kind=kOutput, calls=%fused_computation.21.clone.1 | convolution fusion | flops 3231711232 | bytes 2652164 | tf_op jit(solution)/shard_map/while/body/eval_jaxpr/dot_general | solution.py:24
  89.8 6.4 %fusion.71 = f32[4,512,256]{2,1,0:T(8,128)S(1)} fusion(f32[4,512,256]{2,1,0:T(8,128)S(1)} %get-tuple-element.194, s32[]{:T(128)} %get-tuple-element.193, f32[2048,256]{1,0:T(8,128)} %get-tuple-element.206, f32[2048]{0:T(1024)S(1)} %bitcast.63, f32[512]{0:T(512)S(1)} %bitcast.70, f32[2048]{0:T(1024)S(1)} %bitcast.64, f32[512]{0:T(512)S(1)} %bitcast.69, ...), kind=kOutput, calls=%fused_computation.21.clone.1 | convolution fusion | flops 3231711232 | bytes 2652164 | tf_op jit(solution)/shard_map/while/body/eval_jaxpr/dot_general | solution.py:24
  96.3 6.4 %fusion.71 = f32[4,512,256]{2,1,0:T(8,128)S(1)} fusion(f32[4,512,256]{2,1,0:T(8,128)S(1)} %get-tuple-element.194, s32[]{:T(128)} %get-tuple-element.193, f32[2048,256]{1,0:T(8,128)} %get-tuple-element.206, f32[2048]{0:T(1024)S(1)} %bitcast.63, f32[512]{0:T(512)S(1)} %bitcast.70, f32[2048]{0:T(1024)S(1)} %bitcast.64, f32[512]{0:T(512)S(1)} %bitcast.69, ...), kind=kOutput, calls=%fused_computation.21.clone.1 | convolution fusion | flops 3231711232 | bytes 2652164 | tf_op jit(solution)/shard_map/while/body/eval_jaxpr/dot_general | solution.py:24
  102.7 0.0 copy-start.1
  102.7 0.0 copy-start.2
  102.7 0.0 copy-start.4
  102.7 1.3 copy-done.1
  104.0 0.0 reduce-scatter.3.cloned.1.call-update
  104.1 0.0 all-gather.5.cloned.1.call-start
  104.1 58.5 %reduce-scatter.3.cloned.1.call-done = f32[128,256]{1,0:T(8,128)} async-done(((f32[2048,256]{1,0:T(8,128)}), f32[128,256]{1,0:T(8,128)}) %reduce-scatter.3.cloned.1.call-update) | async-done | bytes 131088 | tf_op jit(solution)/shard_map/reduce_scatter | solution.py:54
  162.6 0.0 copy-done.2
  162.6 0.0 copy-done.4
  162.6 1.0 multiply_reduce_fusion.2
  163.6 79.5 %all-reduce = (f32[256]{0:T(256)S(1)}, f32[256]{0:T(256)S(1)}) all-reduce(f32[256]{0:T(256)S(1)} %get-tuple-element.59, f32[256]{0:T(256)S(1)} %get-tuple-element.58), channel_id=1, replica_groups=mesh['row'=16,'col'=16] {'row','col'}, use_global_device_ids=true, to_apply=%region_1.0 | all-reduce | flops 512 | bytes 4096 | tf_op jit(solution)/shard_map/psum | solution.py:38
  243.1 1.0 multiply_reduce_fusion.1
  244.1 72.5 %psum.30 = f32[256]{0:T(256)S(1)} all-reduce(f32[256]{0:T(256)S(1)} %get-tuple-element.82), channel_id=1, replica_groups=mesh['row'=16,'col'=16] {'row','col'}, use_global_device_ids=true, to_apply=%region_8.9 | all-reduce | flops 256 | bytes 2048 | tf_op jit(solution)/shard_map/psum | solution.py:38
  316.6 0.7 multiply_add_fusion.1
  317.3 0.0 all-gather.5.cloned.1.call-update
  317.3 0.2 reduce-scatter.5.cloned.1.call-start
  317.6 55.1 %all-gather.5.cloned.1.call-done = f32[2048,256]{1,0:T(8,128)} async-done(((f32[128,256]{1,0:T(8,128)}), f32[2048,256]{1,0:T(8,128)}) %all-gather.5.cloned.1.call-update) | async-done | bytes 2097168 | tf_op jit(solution)/shard_map/all_gather | solution.py:53
  372.7 0.2 broadcast.19
  372.9 25.9 %while.21 = (s32[]{:T(128)}, f32[4,512,256]{2,1,0:T(8,128)S(1)}, f32[4,3,512]{2,1,0:T(4,128)S(1)}, f32[3,2048]{1,0:T(4,128)S(1)}, f32[2048,256]{1,0:T(8,128)}, /*index=5*/s32[]{:T(128)}, s32[]{:T(128)}, s32[]{}, s32[]{}) while((s32[]{:T(128)}, f32[4,512,256]{2,1,0:T(8,128)S(1)}, f32[4,3,512]{2,1,0:T(4,128)S(1)}, f32[3,2048]{1,0:T(4,128)S(1)}, ...), condition=%wide.region_10.11_spmd, body=%wide.region_9.10_spmd.sunk | while | flops 3231711232 | bytes 2713733 | solution.py:28
  372.9 6.4 %fusion.75 = f32[4,512,256]{2,1,0:T(8,128)S(1)} fusion(f32[4,512,256]{2,1,0:T(8,128)S(1)} %get-tuple-element.221, s32[]{:T(128)} %get-tuple-element.220, f32[2048,256]{1,0:T(8,128)} %get-tuple-element.233, f32[2048]{0:T(1024)S(1)} %bitcast.66, f32[512]{0:T(512)S(1)} %bitcast.73, f32[2048]{0:T(1024)S(1)} %bitcast.67, f32[512]{0:T(512)S(1)} %bitcast.72, ...), kind=kOutput, calls=%fused_computation.48.clone.1 | convolution fusion | flops 3231711232 | bytes 2652164 | tf_op jit(solution)/shard_map/while/body/eval_jaxpr/dot_general | solution.py:24
  379.4 6.4 %fusion.75 = f32[4,512,256]{2,1,0:T(8,128)S(1)} fusion(f32[4,512,256]{2,1,0:T(8,128)S(1)} %get-tuple-element.221, s32[]{:T(128)} %get-tuple-element.220, f32[2048,256]{1,0:T(8,128)} %get-tuple-element.233, f32[2048]{0:T(1024)S(1)} %bitcast.66, f32[512]{0:T(512)S(1)} %bitcast.73, f32[2048]{0:T(1024)S(1)} %bitcast.67, f32[512]{0:T(512)S(1)} %bitcast.72, ...), kind=kOutput, calls=%fused_computation.48.clone.1 | convolution fusion | flops 3231711232 | bytes 2652164 | tf_op jit(solution)/shard_map/while/body/eval_jaxpr/dot_general | solution.py:24
  385.9 6.4 %fusion.75 = f32[4,512,256]{2,1,0:T(8,128)S(1)} fusion(f32[4,512,256]{2,1,0:T(8,128)S(1)} %get-tuple-element.221, s32[]{:T(128)} %get-tuple-element.220, f32[2048,256]{1,0:T(8,128)} %get-tuple-element.233, f32[2048]{0:T(1024)S(1)} %bitcast.66, f32[512]{0:T(512)S(1)} %bitcast.73, f32[2048]{0:T(1024)S(1)} %bitcast.67, f32[512]{0:T(512)S(1)} %bitcast.72, ...), kind=kOutput, calls=%fused_computation.48.clone.1 | convolution fusion | flops 3231711232 | bytes 2652164 | tf_op jit(solution)/shard_map/while/body/eval_jaxpr/dot_general | solution.py:24
  392.3 6.4 %fusion.75 = f32[4,512,256]{2,1,0:T(8,128)S(1)} fusion(f32[4,512,256]{2,1,0:T(8,128)S(1)} %get-tuple-element.221, s32[]{:T(128)} %get-tuple-element.220, f32[2048,256]{1,0:T(8,128)} %get-tuple-element.233, f32[2048]{0:T(1024)S(1)} %bitcast.66, f32[512]{0:T(512)S(1)} %bitcast.73, f32[2048]{0:T(1024)S(1)} %bitcast.67, f32[512]{0:T(512)S(1)} %bitcast.72, ...), kind=kOutput, calls=%fused_computation.48.clone.1 | convolution fusion | flops 3231711232 | bytes 2652164 | tf_op jit(solution)/shard_map/while/body/eval_jaxpr/dot_general | solution.py:24
  398.7 0.0 copy-start
  398.7 0.0 copy-start.3
  398.8 1.3 copy-done
  400.1 0.0 reduce-scatter.5.cloned.1.call-update
  400.1 61.9 %reduce-scatter.5.cloned.1.call-done = f32[128,256]{1,0:T(8,128)} async-done(((f32[2048,256]{1,0:T(8,128)}), f32[128,256]{1,0:T(8,128)}) %reduce-scatter.5.cloned.1.call-update) | async-done | bytes 131088 | tf_op jit(solution)/shard_map/reduce_scatter | solution.py:54
  462.0 0.0 copy-done.3
  462.0 1.0 multiply_reduce_fusion
  463.0 79.4 %psum.31 = f32[256]{0:T(256)S(1)} all-reduce(f32[256]{0:T(256)S(1)} %multiply_reduce_fusion), channel_id=1, replica_groups=mesh['row'=16,'col'=16] {'row','col'}, use_global_device_ids=true, to_apply=%region_13.14 | all-reduce | flops 256 | bytes 2048 | tf_op jit(solution)/shard_map/psum | solution.py:61
  542.4 1.7 multiply_subtract_fusion
  (19 shorter events, 0.3 us)
Async XLA Ops:
  7.2 69.5 %all-gather.3.cloned.1.call-start = ((), (), s32[]{:S(2)}) async-start(), calls=%async_computation.2 | async-start | bytes 2228224 | tf_op jit(solution)/shard_map/all_gather | solution.py:53
  7.9 154.7 %reduce-scatter.3.cloned.1.call-start = ((), (), s32[]{:S(2)}) async-start(), calls=%async_computation.3 | async-start | bytes 2228224 | tf_op jit(solution)/shard_map/reduce_scatter | solution.py:54
  102.7 1.3 copy-start.1
  102.7 59.9 %copy-start.2 = (f32[128,256]{1,0:T(8,128)S(1)}, f32[128,256]{1,0:T(8,128)}, u32[]{:S(2)}) copy-start(f32[128,256]{1,0:T(8,128)} %param.9) | copy-start | bytes 393220
  102.7 59.9 %copy-start.4 = (f32[128]{0:T(128)S(1)}, f32[128]{0:T(128)}, u32[]{:S(2)}) copy-start(f32[128]{0:T(128)} %param.8) | copy-start | bytes 1540
  104.1 268.6 %all-gather.5.cloned.1.call-start = ((), (), s32[]{:S(2)}) async-start(), calls=%async_computation.4 | async-start | bytes 2228224 | tf_op jit(solution)/shard_map/all_gather | solution.py:53
  317.3 144.7 %reduce-scatter.5.cloned.1.call-start = ((), (), s32[]{:S(2)}) async-start(), calls=%async_computation.5 | async-start | bytes 2228224 | tf_op jit(solution)/shard_map/reduce_scatter | solution.py:54
  398.7 1.3 copy-start
  398.7 63.2 %copy-start.3 = (f32[128,256]{1,0:T(8,128)S(1)}, f32[128,256]{1,0:T(8,128)}, u32[]{:S(2)}) copy-start(f32[128,256]{1,0:T(8,128)} %multiply_add_fusion.1) | copy-start | bytes 393220
Sparse Core Ops, SparseCore 0:
  10.4 62.6 all-gather.2
  104.2 58.3 reduce-scatter.2
  317.4 55.2 all-gather.4
  400.2 61.7 reduce-scatter.4
where the time goes:
time: 551 us
  blocking collectives  300 us (54%)
  waiting for transfers between devices  176 us (32%)
  matrix products  51.2 us (9%)
  between operations  13.8 us (3%)
    psum x2, blocking collectives, squares(): return lax.psum(jnp.sum(residual * residual, axis=0), ('row', 'col'))  152 us
    reduce_scatter x2, waiting for transfers between devices, body(): lax.psum_scatter(kernel_product(row_points, col_points, col_values, kerne...  120 us
    psum x1, blocking collectives, body(): curvature = lax.psum(jnp.sum(direction * image_vec, axis=0), ('row', 'col'))  79.4 us
    all_gather x2, waiting for transfers between devices, body(): col_values = lax.all_gather(direction, 'row', axis=0, tiled=True)  55.1 us
    dot_general x8, matrix products, apply_block(): jnp.dot(weights, values, preferred_element_type=jnp.float32, precision=la...  51.2 us
    all_gather x1, blocking collectives, body(): col_points = lax.all_gather(positions, 'row', axis=1, tiled=True)  40.7 us
    all_gather x1, blocking collectives, body(): row_points = lax.all_gather(positions, 'col', axis=1, tiled=True)  28 us
  transfers between devices with their start and end apart: 4, of which 3 were waited for; matrix products, arithmetic and copies ran while one was open for 0% of the time, Pallas kernels for 0%

commit v1 on v0

--- a/solution.py
+++ b/solution.py
@@ -58,7 +58,9 @@
             tiled=True,
         )
         image_vec = direction / radii[:, None] + summed
-        curvature = lax.psum(jnp.sum(direction * image_vec, axis=0), ("row", "col"))
+        curvature = jnp.sum(
+            lax.all_gather(jnp.sum(direction * image_vec, axis=0), ("row", "col")), axis=0
+        )
         step_size = norm_now / curvature
         solution = solution + step_size * direction
         residual = residual - step_size * image_vec

time: 551 us -> 1160 us (2.11)
  blocking collectives: 300 us -> 909 us
    all_gather x0 -> x2, blocking collectives: none -> 688 us  [body(): lax.all_gather(jnp.sum(direction * image_vec, axis=0), ('row', 'col'))]
    psum x1 -> x0, blocking collectives: 79.4 us -> none  [body(): curvature = lax.psum(jnp.sum(direction * image_vec, axis=0), ('row', 'col'))]
where the time goes in v1:
time: 1160 us
  blocking collectives  909 us (78%)
  waiting for transfers between devices  176 us (15%)
  matrix products  51.2 us (4%)
  between operations  13.8 us (1%)
    all_gather x2, blocking collectives, body(): lax.all_gather(jnp.sum(direction * image_vec, axis=0), ('row', 'col'))  688 us
    psum x2, blocking collectives, squares(): return lax.psum(jnp.sum(residual * residual, axis=0), ('row', 'col'))  152 us
    reduce_scatter x2, waiting for transfers between devices, body(): lax.psum_scatter(kernel_product(row_points, col_points, col_values, kerne...  120 us
    all_gather x2, waiting for transfers between devices, body(): col_values = lax.all_gather(direction, 'row', axis=0, tiled=True)  55.4 us
    dot_general x8, matrix products, apply_block(): jnp.dot(weights, values, preferred_element_type=jnp.float32, precision=la...  51.2 us
    all_gather x1, blocking collectives, body(): col_points = lax.all_gather(positions, 'row', axis=1, tiled=True)  40.7 us
    all_gather x1, blocking collectives, body(): row_points = lax.all_gather(positions, 'col', axis=1, tiled=True)  28 us
  transfers between devices with their start and end apart: 4, of which 3 were waited for; matrix products, arithmetic and copies ran while one was open for 0% of the time, Pallas kernels for 0%

profile of v1, /device:TPU:1, one launch (start us, length us, event | category | flops | bytes accessed | tf_op | source)
XLA Modules:
  0.0 1160.3 jit_solution(4004648520338470616)
XLA Ops:
  7.2 0.0 all-gather.7.cloned.1.call-start
  7.2 0.7 all-gather.7.cloned.1.call-update
  7.9 0.0 reduce-scatter.3.cloned.1.call-start
  7.9 40.7 %all_gather.25 = f32[3,2048]{1,0:T(4,128)S(1)} all-gather(f32[3,128]{1,0:T(4,128)} %param.7), channel_id=1, replica_groups=mesh['row'=16,'col'=16] {'row'}, dimensions={1}, use_global_device_ids=true | all-gather | bytes 26112 | tf_op jit(solution)/shard_map/all_gather | solution.py:46
  48.7 28.0 %all_gather.24 = f32[3,2048]{1,0:T(4,128)S(1)} all-gather(f32[3,128]{1,0:T(4,128)} %param.7), channel_id=1, replica_groups=mesh['row'=16,'col'=16] {'col'}, dimensions={1}, use_global_device_ids=true | all-gather | bytes 26112 | tf_op jit(solution)/shard_map/all_gather | solution.py:45
  76.6 0.0 all-gather.7.cloned.1.call-done
  76.6 0.2 broadcast.19.clone
  76.8 25.9 %while.20 = (s32[]{:T(128)}, f32[4,512,256]{2,1,0:T(8,128)S(1)}, f32[4,3,512]{2,1,0:T(4,128)S(1)}, f32[3,2048]{1,0:T(4,128)S(1)}, f32[2048,256]{1,0:T(8,128)}, /*index=5*/s32[]{:T(128)}, s32[]{:T(128)}, s32[]{}, s32[]{}) while((s32[]{:T(128)}, f32[4,512,256]{2,1,0:T(8,128)S(1)}, f32[4,3,512]{2,1,0:T(4,128)S(1)}, f32[3,2048]{1,0:T(4,128)S(1)}, ...), condition=%wide.region_3.4_spmd, body=%wide.region_2.3_spmd.sunk | while | flops 3231711232 | bytes 2713733 | solution.py:28
  76.8 6.4 fusion.71
  83.3 6.4 fusion.71
  89.8 6.4 fusion.71
  96.3 6.4 fusion.71
  102.7 0.0 copy-start
  102.7 0.0 copy-start.2
  102.7 0.0 copy-start.4
  102.7 1.3 copy-done
  104.0 0.0 reduce-scatter.3.cloned.1.call-update
  104.1 0.0 all-gather.9.cloned.1.call-start
  104.1 58.5 %reduce-scatter.3.cloned.1.call-done = f32[128,256]{1,0:T(8,128)} async-done(((f32[2048,256]{1,0:T(8,128)}), f32[128,256]{1,0:T(8,128)}) %reduce-scatter.3.cloned.1.call-update) | async-done | bytes 131088 | tf_op jit(solution)/shard_map/reduce_scatter | solution.py:54
  162.6 0.0 copy-done.2
  162.6 0.0 copy-done.4
  162.6 1.0 multiply_reduce_fusion.2
  163.6 79.5 %psum.14 = f32[256]{0:T(256)S(1)} all-reduce(f32[256]{0:T(256)S(1)} %get-tuple-element.59), channel_id=1, replica_groups=mesh['row'=16,'col'=16] {'row','col'}, use_global_device_ids=true, to_apply=%region_1.0 | all-reduce | flops 256 | bytes 2048 | tf_op jit(solution)/shard_map/psum | solution.py:38
  243.1 341.4 %all-gather.2 = f32[256,1,256]{2,1,0:T(1,128)S(1)} all-gather(f32[1,1,256]{2,1,0:T(1,128)S(1)} %bitcast.76), channel_id=2, replica_groups=mesh['row'=16,'col'=16] {'row','col'}, dimensions={0}, use_global_device_ids=true | all-gather | bytes 263168 | tf_op jit(solution)/shard_map/all_gather | solution.py:62
  584.5 0.3 reduce_sum.56
  584.8 1.0 multiply_reduce_fusion.1
  585.8 72.7 %psum.15 = f32[256]{0:T(256)S(1)} all-reduce(f32[256]{0:T(256)S(1)} %get-tuple-element.80), channel_id=1, replica_groups=mesh['row'=16,'col'=16] {'row','col'}, use_global_device_ids=true, to_apply=%region_8.9 | all-reduce | flops 256 | bytes 2048 | tf_op jit(solution)/shard_map/psum | solution.py:38
  658.5 0.7 multiply_add_fusion.1
  659.2 0.0 all-gather.9.cloned.1.call-update
  659.2 0.2 reduce-scatter.5.cloned.1.call-start
  659.5 55.4 %all-gather.9.cloned.1.call-done = f32[2048,256]{1,0:T(8,128)} async-done(((f32[128,256]{1,0:T(8,128)}), f32[2048,256]{1,0:T(8,128)}) %all-gather.9.cloned.1.call-update) | async-done | bytes 2097168 | tf_op jit(solution)/shard_map/all_gather | solution.py:53
  714.8 0.2 broadcast.19
  715.0 25.9 %while.21 = (s32[]{:T(128)}, f32[4,512,256]{2,1,0:T(8,128)S(1)}, f32[4,3,512]{2,1,0:T(4,128)S(1)}, f32[3,2048]{1,0:T(4,128)S(1)}, f32[2048,256]{1,0:T(8,128)}, /*index=5*/s32[]{:T(128)}, s32[]{:T(128)}, s32[]{}, s32[]{}) while((s32[]{:T(128)}, f32[4,512,256]{2,1,0:T(8,128)S(1)}, f32[4,3,512]{2,1,0:T(4,128)S(1)}, f32[3,2048]{1,0:T(4,128)S(1)}, ...), condition=%wide.region_10.11_spmd, body=%wide.region_9.10_spmd.sunk | while | flops 3231711232 | bytes 2713733 | solution.py:28
  715.0 6.4 fusion.75
  721.5 6.4 fusion.75
  728.0 6.4 fusion.75
  734.4 6.4 fusion.75
  740.9 0.0 copy-start.1
  740.9 0.0 copy-start.3
  740.9 1.3 copy-done.1
  742.2 0.0 reduce-scatter.5.cloned.1.call-update
  742.2 61.9 %reduce-scatter.5.cloned.1.call-done = f32[128,256]{1,0:T(8,128)} async-done(((f32[2048,256]{1,0:T(8,128)}), f32[128,256]{1,0:T(8,128)}) %reduce-scatter.5.cloned.1.call-update) | async-done | bytes 131088 | tf_op jit(solution)/shard_map/reduce_scatter | solution.py:54
  804.1 0.0 copy-done.3
  804.1 1.0 multiply_reduce_fusion
  805.1 346.6 %all-gather.3 = f32[256,1,256]{2,1,0:T(1,128)S(1)} all-gather(f32[1,1,256]{2,1,0:T(1,128)S(1)} %bitcast.77), channel_id=3, replica_groups=mesh['row'=16,'col'=16] {'row','col'}, dimensions={0}, use_global_device_ids=true | all-gather | bytes 263168 | tf_op jit(solution)/shard_map/all_gather | solution.py:62
  1151.8 0.3 reduce_sum.59
  1152.1 1.7 multiply_subtract_fusion
  (19 shorter events, 0.3 us)
Async XLA Ops:
  7.2 69.5 %all-gather.7.cloned.1.call-start = ((), (), s32[]{:S(2)}) async-start(), calls=%async_computation.2 | async-start | bytes 2228224 | tf_op jit(solution)/shard_map/all_gather | solution.py:53
  7.9 154.7 %reduce-scatter.3.cloned.1.call-start = ((), (), s32[]{:S(2)}) async-start(), calls=%async_computation.3 | async-start | bytes 2228224 | tf_op jit(solution)/shard_map/reduce_scatter | solution.py:54
  102.7 1.4 copy-start
  102.7 59.9 %copy-start.2 = (f32[128,256]{1,0:T(8,128)S(1)}, f32[128,256]{1,0:T(8,128)}, u32[]{:S(2)}) copy-start(f32[128,256]{1,0:T(8,128)} %param.9) | copy-start | bytes 393220
  102.7 59.9 %copy-start.4 = (f32[128]{0:T(128)S(1)}, f32[128]{0:T(128)}, u32[]{:S(2)}) copy-start(f32[128]{0:T(128)} %param.8) | copy-start | bytes 1540
  104.1 610.8 %all-gather.9.cloned.1.call-start = ((), (), s32[]{:S(2)}) async-start(), calls=%async_computation.4 | async-start | bytes 2228224 | tf_op jit(solution)/shard_map/all_gather | solution.py:53
  659.2 144.9 %reduce-scatter.5.cloned.1.call-start = ((), (), s32[]{:S(2)}) async-start(), calls=%async_computation.5 | async-start | bytes 2228224 | tf_op jit(solution)/shard_map/reduce_scatter | solution.py:54
  740.9 1.4 copy-start.1
  740.9 63.3 %copy-start.3 = (f32[128,256]{1,0:T(8,128)S(1)}, f32[128,256]{1,0:T(8,128)}, u32[]{:S(2)}) copy-start(f32[128,256]{1,0:T(8,128)} %multiply_add_fusion.1) | copy-start | bytes 393220
Sparse Core Ops, SparseCore 0:
  10.4 62.6 all-gather.6
  104.2 58.3 reduce-scatter.2
  659.3 55.4 all-gather.8
  742.4 61.7 reduce-scatter.4
